TPU v7x, 32 devices: a whole 2x2x4 slice. The times are simulated.
32 devices in a mesh: ctx: 8 (over z, y), chan: 4 (over x, core).
Axes of the slice: x: 2, y: 2, z: 4, core: 2. Of those that a mesh axis runs over, the one named last changes fastest.
Arguments:
- tokens: bfloat16 [2048, 4096], P('ctx', 'chan'), may hold values from -6 to 6
- gain: float32 [4096], replicated, may hold values from 0.1 to 1.9
- in_weight: bfloat16 [3, 4096, 2048], P(None, None, 'chan'), may hold values from -0.09375 to 0.09375
- short_weight: float32 [3, 3, 2048], P(None, None, 'chan'), may hold values from -3.5 to 3.5
- residues: float32 [16, 2048], P(None, 'chan'), may hold values from -1.5 to 1.5
- rates: float32 [16, 2048], P(None, 'chan'), may hold values from 0.1 to 51
- out_weight: bfloat16 [2048, 4096], P('chan'), may hold values from -0.1875 to 0.1875
Outputs:
- mixed: bfloat16 [2048, 4096], P('ctx', 'chan')
All inputs are finite; a program needn't handle non-finite values.
Results may differ from a plain program's by a relative error of at most 0.018.
Values may be sent and summed in bfloat16 or wider, within the bound.
A program may use at most 128 MiB of HBM per device.

v0:
```python
import math
import jax
import jax.numpy as jnp
from jax import lax
from jax.sharding import PartitionSpec as P

highest = lax.Precision.HIGHEST
two_pi = 2.0 * math.pi


def shortened(shard):

    def short(part):
        return part.astype(jnp.bfloat16) if part.dtype == jnp.float32 else part

    return jax.tree.map(short, shard)


def from_behind(shard, axis, by):
    peers = lax.axis_size(axis)
    pairs = [(i, i + by) for i in range(peers) if 0 <= i + by < peers]
    return lax.ppermute(shard, axis, pairs)


def turn_angle(first, second, modulus):
    return (first * second % modulus).astype(jnp.float32) * (two_pi / modulus)


def local_forward(spectra, freq_slots, padded_length):
    row_count = spectra.shape[3]
    steps_idx = jnp.arange(row_count, dtype=jnp.int32)
    twiddle = turn_angle(freq_slots[:, None], steps_idx[None, :], padded_length)[:, :, None]
    cosine_term = jnp.cos(twiddle)
    sine_term = jnp.sin(twiddle)
    real_part = spectra[:, 0]
    imag_part = spectra[:, 1]
    turned_real = real_part * cosine_term + imag_part * sine_term
    turned_imag = imag_part * cosine_term - real_part * sine_term
    stacked = jnp.concatenate([turned_real, turned_imag], axis=2)
    dft_angle = turn_angle(steps_idx[:, None], steps_idx[None, :], row_count)
    cos_table = jnp.cos(dft_angle)
    sin_table = jnp.sin(dft_angle)
    block_table = jnp.concatenate(
        [
            jnp.concatenate([cos_table, sin_table], axis=1),
            jnp.concatenate([-sin_table, cos_table], axis=1),
        ],
        axis=0,
    )
    both_parts = jnp.einsum("pj,fsjc->fspc", block_table, stacked, precision=highest)
    return (both_parts[:, :, :row_count], both_parts[:, :, row_count:])


def local_inverse(spec_real, spec_imag, freq_slots, padded_length):
    row_count = spec_real.shape[1]
    steps_idx = jnp.arange(row_count, dtype=jnp.int32)
    dft_angle = turn_angle(steps_idx[:, None], steps_idx[None, :], row_count)
    cos_table = jnp.cos(dft_angle)
    sin_table = jnp.sin(dft_angle)
    block_table = jnp.concatenate(
        [
            jnp.concatenate([cos_table, -sin_table], axis=1),
            jnp.concatenate([sin_table, cos_table], axis=1),
        ],
        axis=0,
    )
    stacked = jnp.concatenate([spec_real, spec_imag], axis=1)
    both_parts = jnp.einsum("jp,spc->sjc", block_table, stacked, precision=highest) / row_count
    back_real = both_parts[:, :row_count]
    back_imag = both_parts[:, row_count:]
    twiddle = turn_angle(freq_slots[:, None], steps_idx[None, :], padded_length)[:, :, None]
    cosine_term = jnp.cos(twiddle)
    sine_term = jnp.sin(twiddle)
    return (
        back_real * cosine_term - back_imag * sine_term,
        back_imag * cosine_term + back_real * sine_term,
    )


def across_blocks(received, sample_ids, freq_count):
    freq_ids = jnp.arange(freq_count, dtype=jnp.int32)
    rotation = turn_angle(freq_ids[:, None], sample_ids[None, :], freq_count)
    real_part = jnp.einsum("qm,fmjc->fqjc", jnp.cos(rotation), received, precision=highest)
    imag_part = -jnp.einsum("qm,fmjc->fqjc", jnp.sin(rotation), received, precision=highest)
    return jnp.stack([real_part, imag_part], axis=1)


def rows_from_spectra(received, sample_ids, freq_count):
    freq_ids = jnp.arange(freq_count, dtype=jnp.int32)
    rotation = turn_angle(sample_ids[:, None], freq_ids[None, :], freq_count)
    real_rows = jnp.einsum("mq,qjc->mjc", jnp.cos(rotation), received[0], precision=highest)
    real_rows = real_rows - jnp.einsum(
        "mq,qjc->mjc", jnp.sin(rotation), received[1], precision=highest
    )
    return real_rows / freq_count


def halved_forward(signal, device_index, group_size):
    received = lax.all_to_all(
        signal[:, None].astype(jnp.bfloat16), "ctx", split_axis=2, concat_axis=1, tiled=True
    ).astype(jnp.float32)
    spectra = across_blocks(received, jnp.arange(group_size, dtype=jnp.int32), 2 * group_size)
    gathered = lax.all_to_all(
        shortened(spectra), "ctx", split_axis=2, concat_axis=3, tiled=True
    ).astype(spectra.dtype)
    return (gathered, 2 * device_index + jnp.arange(2, dtype=jnp.int32))


def halved_inverse(spec_real, spec_imag, group_size):
    received = lax.all_to_all(
        shortened(jnp.stack([spec_real, spec_imag], axis=0)),
        "ctx",
        split_axis=2,
        concat_axis=1,
        tiled=True,
    )
    real_rows = rows_from_spectra(received, jnp.arange(group_size, dtype=jnp.int32), 2 * group_size)
    returned = lax.all_to_all(
        shortened(real_rows), "ctx", split_axis=0, concat_axis=1, tiled=True
    ).astype(real_rows.dtype)
    return returned[0]


def shards(tokens, gain, in_weight, short_weight, residues, rates, out_weight):
    features_all = lax.all_gather(tokens, "chan", axis=1, tiled=True)
    wide_rows = features_all.astype(jnp.float32)
    scale_rms = lax.rsqrt(jnp.mean(wide_rows * wide_rows, axis=-1, keepdims=True) + 1e-06)
    normed = (wide_rows * scale_rms * gain).astype(jnp.bfloat16)
    projected = jnp.einsum(
        "td,gdc->gtc", normed, in_weight, preferred_element_type=jnp.float32
    ).astype(jnp.bfloat16)
    row_count = projected.shape[1]
    rim_size = short_weight.shape[1] - 1
    rim_rows = from_behind(projected[:, row_count - rim_size :, :], "ctx", 1)
    extended = jnp.concatenate([rim_rows, projected], axis=1).astype(jnp.float32)
    filtered = jnp.zeros((3, row_count, projected.shape[2]), jnp.float32)
    for i in range(rim_size + 1):
        filtered = (
            filtered
            + short_weight[:, i][:, None, :] * extended[:, rim_size - i : rim_size - i + row_count]
        )
    drive_term = filtered[1] * filtered[2]
    group_size = lax.axis_size("ctx")
    device_index = lax.axis_index("ctx")
    length = row_count * group_size
    padded_length = 2 * length
    decay_rate = rates / length
    amplitude = residues * jnp.sqrt(-jnp.expm1(-2.0 * decay_rate))
    positions = (device_index * row_count + jnp.arange(row_count, dtype=jnp.int32)).astype(
        jnp.float32
    )
    kernel = jnp.sum(
        amplitude[:, None, :] * jnp.exp(-decay_rate[:, None, :] * positions[None, :, None]), axis=0
    )
    signal = jnp.stack([drive_term, kernel], axis=0)
    spectra, freq_slots = halved_forward(signal, device_index, group_size)
    spec_real, spec_imag = local_forward(spectra, freq_slots, padded_length)
    resp_real = spec_real[1]
    resp_imag = spec_imag[1]
    prod_real = spec_real[0] * resp_real - spec_imag[0] * resp_imag
    prod_imag = spec_real[0] * resp_imag + spec_imag[0] * resp_real
    back_real, back_imag = local_inverse(prod_real, prod_imag, freq_slots, padded_length)
    convolved = halved_inverse(back_real, back_imag, group_size)
    gated_rows = (filtered[0] * convolved).astype(jnp.bfloat16)
    partial_sums = jnp.dot(gated_rows, out_weight, preferred_element_type=jnp.float32)
    return lax.psum_scatter(
        partial_sums.astype(jnp.bfloat16), "chan", scatter_dimension=1, tiled=True
    )


def solution(mesh):
    return jax.shard_map(
        shards,
        mesh=mesh,
        in_specs=(
            P("ctx", "chan"),
            P(),
            P(None, None, "chan"),
            P(None, None, "chan"),
            P(None, "chan"),
            P(None, "chan"),
            P("chan", None),
        ),
        out_specs=P("ctx", "chan"),
        check_vma=False,
    )
```

profile of v0, /device:TPU:0, one launch (start us, length us, event | category | flops | bytes accessed | tf_op | source)
XLA Modules:
  0.0 229.2 jit_solution(4837787021221969557)
XLA Ops:
  6.5 0.7 all-gather.2.cloned.1.call-update
  7.3 0.9 fusion.110
  8.1 0.8 sqrt_multiply_fusion
  9.0 1.4 multiply_reduce_fusion
  10.4 23.8 %all-gather.2.cloned.1.call-done = bf16[256,4096]{1,0:T(8,128)(2,1)} async-done(((bf16[256,1024]{1,0:T(8,128)(2,1)}), bf16[256,4096]{1,0:T(8,128)(2,1)}) %all-gather.2.cloned.1.call-update) | async-done | bytes 2097168 | tf_op jit(solution)/shard_map/all_gather | solution.py:125
  34.2 2.2 fusion
  36.5 6.6 %fusion.28 = bf16[3,256,512]{2,1,0:T(8,128)(2,1)S(1)} fusion(bf16[3,4096,512]{2,1,0:T(8,128)(2,1)} %param.9, bf16[256,4096]{1,0:T(8,128)(2,1)S(1)} %copy-done.2, f32[4096]{0:T(1024)S(1)} %copy-done.3, f32[256]{0:T(256)S(1)} %add_rsqrt_fusion), kind=kOutput, calls=%fused_computation.40 | convolution fusion | flops 3225812992 | bytes 15483904 | tf_op jit(solution)/shard_map/td,gdc->gtc/dot_general | solution.py:129
  43.1 3.4 %collective-permute-start = (bf16[3,2,512]{2,1,0:T(2,128)(2,1)S(1)}, bf16[3,2,512]{2,1,0:T(2,128)(2,1)S(1)}, u32[]{:S(2)}, u32[]{:S(2)}) collective-permute-start(bf16[3,2,512]{2,1,0:T(2,128)(2,1)S(1)} %slice.90), channel_id=1, source_target_pairs={{0,4},{4,8},{8,12},{12,16},{16,20},{20,24},{24,28},{1,5},{5,9},{9,... | collective-permute-start | bytes 18440 | tf_op jit(solution)/shard_map/ppermute | solution.py:22
  46.5 1.3 collective-permute-done
  48.1 0.5 fusion.21
  48.7 0.5 copy.56
  49.2 19.9 %all_to_all.45 = bf16[2,1,256,512]{3,0,1,2:T(2,128)(2,1)S(1)} all-to-all(bf16[2,1,256,512]{3,0,1,2:T(2,128)(2,1)S(1)} %copy.56), channel_id=1, replica_groups=mesh['ctx'=8,'chan'=4] {'ctx'}, dimensions={2} | all-to-all | bytes 1048576 | tf_op jit(solution)/shard_map/all_to_all | solution.py:99
  69.2 1.1 fusion.26
  70.3 1.1 fusion.27
  71.6 2.5 %copy.60 = bf16[2,2,16,32,512]{4,3,0,1,2:T(8,128)(2,1)} copy(bf16[2,2,16,32,512]{4,2,3,0,1:T(8,128)(2,1)S(1)} %pad_maximum_fusion) | data formatting | bytes 4194304 | tf_op jit(solution)/shard_map/stack | solution.py:85
  74.1 3.6 %all-to-all-start.1 = ((bf16[2,2,16,32,512]{4,3,0,1,2:T(8,128)(2,1)}), bf16[2,2,16,32,512]{4,3,0,1,2:T(8,128)(2,1)S(1)}, u32[]{:S(2)}, u32[]{:S(2)}) async-start(bf16[2,2,16,32,512]{4,3,0,1,2:T(8,128)(2,1)} %copy.60), calls=%async_computation.1 | async-start | bytes 4194304 | tf_op jit(solution)/shard_map/all_to_all | solution.py:103
  78.0 1.0 fusion.60
  79.0 1.0 fusion.58
  80.2 45.4 %all-to-all-done.1 = bf16[2,2,16,32,512]{4,3,0,1,2:T(8,128)(2,1)S(1)} async-done(((bf16[2,2,16,32,512]{4,3,0,1,2:T(8,128)(2,1)}), bf16[2,2,16,32,512]{4,3,0,1,2:T(8,128)(2,1)S(1)}, u32[]{:S(2)}, u32[]{:S(2)}) %all-to-all-start.1) | async-done | bytes 2097184 | tf_op jit(solution)/shard_map/all_to_all | solution.py:103
  125.5 0.6 copy.61
  126.1 0.5 multiply_add_fusion
  126.6 7.9 %fusion.7 = f32[2,2,512,512]{3,2,1,0:T(8,128)S(1)} fusion(f32[2,2,256,512]{3,2,1,0:T(8,128)S(1)} %get-tuple-element.6, f32[2,2,256,512]{3,2,1,0:T(8,128)S(1)} %get-tuple-element.5, f32[256,256]{1,0:T(8,128)S(1)} %get-tuple-element.23, f32[256,256]{1,0:T(8,128)S(1)} %fusion.60, f32[256,256]{1,0:T(8,128)S(1)} %get-tuple-element.22), kind=kOutput, calls=%fused_computation.11 | convolution fusion | flops 6444285952 | bytes 9175040 | tf_op jit(solution)/shard_map/pj,fsjc->fspc/dot_general | solution.py:50
  134.6 0.5 subtract_bitcast_fusion
  135.1 7.1 %multiply_bitcast_fusion = f32[2,512,512]{1,2,0:T(8,128)S(1)} fusion(f32[2,256,512]{2,1,0:T(8,128)S(1)} %get-tuple-element.8, f32[2,256,512]{2,1,0:T(8,128)S(1)} %get-tuple-element.7, f32[256,256]{1,0:T(8,128)S(1)} %get-tuple-element.23, f32[256,256]{1,0:T(8,128)S(1)} %get-tuple-element.22, f32[256,256]{1,0:T(8,128)S(1)} %fusion.60), kind=kOutput, calls=%fused_computation.21 | convolution fusion | flops 3223060480 | bytes 4980736 | tf_op jit(solution)/shard_map/jp,spc->sjc/dot_general | solution.py:68
  142.6 1.1 copy.63
  143.7 29.3 %all_to_all.46 = bf16[2,2,256,512]{3,1,0,2:T(2,128)(2,1)S(1)} all-to-all(bf16[2,2,256,512]{3,1,0,2:T(2,128)(2,1)S(1)} %copy.63), channel_id=1, replica_groups=mesh['ctx'=8,'chan'=4] {'ctx'}, dimensions={2} | all-to-all | bytes 2097152 | tf_op jit(solution)/shard_map/all_to_all | solution.py:110
  173.4 0.5 copy.65
  174.6 0.5 copy.66
  175.3 0.4 fusion.32
  175.8 12.0 %all_to_all.47 = bf16[8,32,512]{2,1,0:T(8,128)(2,1)S(1)} all-to-all(bf16[8,32,512]{2,1,0:T(8,128)(2,1)S(1)} %copy.67), channel_id=1, replica_groups=mesh['ctx'=8,'chan'=4] {'ctx'}, dimensions={0} | all-to-all | bytes 524288 | tf_op jit(solution)/shard_map/all_to_all | solution.py:118
  187.8 4.8 %convolution_convert_fusion = bf16[256,4096]{1,0:T(8,128)(2,1)} fusion(bf16[512,4096]{1,0:T(8,128)(2,1)} %param.13, f32[3,256,512]{2,1,0:T(8,128)S(1)} %copy-done.1, bf16[256,512]{1,0:T(8,128)(2,1)S(1)} %bitcast.108), kind=kOutput, calls=%fused_computation.3 | convolution fusion | flops 1075183616 | bytes 7077888 | tf_op jit(solution)/shard_map/dot_general | solution.py:165
  192.6 29.7 %reduce-scatter.2.cloned.1.call-done = bf16[256,1024]{1,0:T(8,128)(2,1)} async-done(((bf16[256,4096]{1,0:T(8,128)(2,1)}), bf16[256,1024]{1,0:T(8,128)(2,1)}) %reduce-scatter.2.cloned.1.call-update) | async-done | bytes 524304 | tf_op jit(solution)/shard_map/reduce_scatter | solution.py:166
  (31 shorter events, 2.6 us)
Async XLA Ops:
  6.5 27.7 %all-gather.2.cloned.1.call-start = ((), (), s32[]{:S(2)}) async-start(), calls=%async_computation.5 | async-start | bytes 2621440 | tf_op jit(solution)/shard_map/all_gather | solution.py:125
  9.0 27.5 %copy-start.3 = (f32[4096]{0:T(1024)S(1)}, f32[4096]{0:T(1024)}, u32[]{:S(2)}) copy-start(f32[4096]{0:T(1024)} %param.8) | copy-start | bytes 49156
  34.2 2.3 copy-start.2
  43.1 4.7 %collective-permute-start = (bf16[3,2,512]{2,1,0:T(2,128)(2,1)S(1)}, bf16[3,2,512]{2,1,0:T(2,128)(2,1)S(1)}, u32[]{:S(2)}, u32[]{:S(2)}) collective-permute-start(bf16[3,2,512]{2,1,0:T(2,128)(2,1)S(1)} %slice.90), channel_id=1, source_target_pairs={{0,4},{4,8},{8,12},{12,16},{16,20},{20,24},{24,28},{1,5},{5,9},{9,... | collective-permute-start | bytes 18440 | tf_op jit(solution)/shard_map/ppermute | solution.py:22
  48.5 20.6 %copy-start = (f32[3,256,512]{2,1,0:T(8,128)}, f32[3,256,512]{2,1,0:T(8,128)S(1)}, u32[]{:S(2)}) copy-start(f32[3,256,512]{2,1,0:T(8,128)S(1)} %fusion.21) | copy-start | bytes 4718596
  74.1 51.4 %all-to-all-start.1 = ((bf16[2,2,16,32,512]{4,3,0,1,2:T(8,128)(2,1)}), bf16[2,2,16,32,512]{4,3,0,1,2:T(8,128)(2,1)S(1)}, u32[]{:S(2)}, u32[]{:S(2)}) async-start(bf16[2,2,16,32,512]{4,3,0,1,2:T(8,128)(2,1)} %copy.60), calls=%async_computation.1 | async-start | bytes 4194304 | tf_op jit(solution)/shard_map/all_to_all | solution.py:103
  77.8 144.6 %reduce-scatter.2.cloned.1.call-start = ((), (), s32[]{:S(2)}) async-start(), calls=%async_computation.6 | async-start | bytes 2621440 | tf_op jit(solution)/shard_map/reduce_scatter | solution.py:166
  174.6 13.3 %copy-start.1 = (f32[3,256,512]{2,1,0:T(8,128)S(1)}, f32[3,256,512]{2,1,0:T(8,128)}, u32[]{:S(2)}) copy-start(f32[3,256,512]{2,1,0:T(8,128)} %copy-done) | copy-start | bytes 4718596
Sparse Core Ops, SparseCore 0:
  8.9 25.2 all-gather.1
  192.8 29.5 reduce-scatter.1
where the time goes:
time: 230 us; the launch traced here: 229 us
  waiting for transfers between devices  101 us (44%)
  blocking collectives  61.2 us (27%)
  matrix products  29.5 us (13%)
  between operations  13.7 us (6%)
  other arithmetic  9.09 us (4%)
  local copies, waits for them, and re-layouts  7.54 us (3%)
  starting transfers between devices  7.23 us (3%)
    all_to_all x1, waiting for transfers between devices, halved_forward(): lax.all_to_all(shortened(spectra), 'ctx', split_axis=2, concat_axis=3, ti...  45.4 us
    reduce_scatter x1, waiting for transfers between devices, shards(): lax.psum_scatter(partial_sums.astype(jnp.bfloat16), 'chan', scatter_dimen...  29.7 us
    all_to_all x1, blocking collectives, halved_inverse(): lax.all_to_all(shortened(jnp.stack([spec_real, spec_imag], axis=0)), 'ctx...  29.3 us
    all_gather x1, waiting for transfers between devices, shards(): features_all = lax.all_gather(tokens, 'chan', axis=1, tiled=True)  23.8 us
    all_to_all x1, blocking collectives, halved_forward(): lax.all_to_all(signal[:, None].astype(jnp.bfloat16), 'ctx', split_axis=2,...  19.9 us
    all_to_all x1, blocking collectives, halved_inverse(): lax.all_to_all(shortened(real_rows), 'ctx', split_axis=0, concat_axis=1,...  12 us
    dot_general x1, matrix products, local_forward(): jnp.einsum('pj,fsjc->fspc', block_table, stacked, precision=highest)  7.95 us
    dot_general x1, matrix products, local_inverse(): jnp.einsum('jp,spc->sjc', block_table, stacked, precision=highest)  7.1 us
  transfers between devices with their start and end apart: 4, of which 4 were waited for; matrix products, arithmetic and copies ran while one was open for 2% of the time, Pallas kernels for 0%

commit v1 on v0

--- a/solution.py
+++ b/solution.py
@@ -107,12 +107,20 @@
 
 
 def halved_inverse(spec_real, spec_imag, group_size):
-    received = lax.all_to_all(
-        shortened(jnp.stack([spec_real, spec_imag], axis=0)),
-        "ctx",
-        split_axis=2,
-        concat_axis=1,
-        tiled=True,
+    received = jnp.concatenate(
+        lax.all_to_all(
+            jnp.stack(
+                jnp.split(
+                    shortened(jnp.stack([spec_real, spec_imag], axis=0)),
+                    lax.axis_size("ctx"),
+                    axis=2,
+                )
+            ),
+            "ctx",
+            0,
+            0,
+        ),
+        axis=1,
     )
     real_rows = rows_from_spectra(received, jnp.arange(group_size, dtype=jnp.int32), 2 * group_size)
     returned = lax.all_to_all(

time: 230 us -> 222 us (0.965)
  matrix products: 29.5 us -> 24.4 us
  local copies, waits for them, and re-layouts: 7.54 us -> 4.77 us
    dot_general x1, matrix products: 7.1 us -> 3.78 us  [local_inverse(): jnp.einsum('jp,spc->sjc', block_table, stacked, precision=highest)]
where the time goes in v1:
time: 222 us
  waiting for transfers between devices  101 us (45%)
  blocking collectives  61.5 us (28%)
  matrix products  24.4 us (11%)
  between operations  13.7 us (6%)
  other arithmetic  9.08 us (4%)
  starting transfers between devices  7.23 us (3%)
  local copies, waits for them, and re-layouts  4.77 us (2%)
    all_to_all x1, waiting for transfers between devices, halved_forward(): lax.all_to_all(shortened(spectra), 'ctx', split_axis=2, concat_axis=3, ti...  45.4 us
    reduce_scatter x1, waiting for transfers between devices, shards(): lax.psum_scatter(partial_sums.astype(jnp.bfloat16), 'chan', scatter_dimen...  29.6 us
    all_to_all x1, blocking collectives, halved_inverse(): lax.all_to_all(jnp.stack(jnp.split(shortened(jnp.stack([spec_real, spec_i...  29.6 us
    all_gather x1, waiting for transfers between devices, shards(): features_all = lax.all_gather(tokens, 'chan', axis=1, tiled=True)  23.8 us
    all_to_all x1, blocking collectives, halved_forward(): lax.all_to_all(signal[:, None].astype(jnp.bfloat16), 'ctx', split_axis=2,...  19.9 us
    all_to_all x1, blocking collectives, halved_inverse(): lax.all_to_all(shortened(real_rows), 'ctx', split_axis=0, concat_axis=1,...  12 us
    dot_general x1, matrix products, local_forward(): jnp.einsum('pj,fsjc->fspc', block_table, stacked, precision=highest)  7.95 us
    dot_general x1, matrix products, shards(): jnp.einsum('td,gdc->gtc', normed, in_weight, preferred_element_type=jnp.f...  6.59 us
  transfers between devices with their start and end apart: 4, of which 4 were waited for; matrix products, arithmetic and copies ran while one was open for 2% of the time, Pallas kernels for 0%

profile of v1, /device:TPU:0, one launch (start us, length us, event | category | flops | bytes accessed | tf_op | source)
XLA Modules:
  0.0 221.6 jit_solution(15538116923086063474)
XLA Ops:
  6.5 0.7 all-gather.2.cloned.1.call-update
  7.3 0.9 fusion.121
  8.1 0.8 sqrt_multiply_fusion
  9.0 1.4 multiply_reduce_fusion
  10.4 23.8 %all-gather.2.cloned.1.call-done = bf16[256,4096]{1,0:T(8,128)(2,1)} async-done(((bf16[256,1024]{1,0:T(8,128)(2,1)}), bf16[256,4096]{1,0:T(8,128)(2,1)}) %all-gather.2.cloned.1.call-update) | async-done | bytes 2097168 | tf_op jit(solution)/shard_map/all_gather | solution.py:133
  34.2 2.2 %fusion = f32[256]{0:T(256)S(1)} fusion(bf16[256,4096]{1,0:T(8,128)(2,1)} %all-gather.2.cloned.1.call-done), kind=kLoop, calls=%fused_computation.4 | loop fusion | flops 3145472 | bytes 2098176 | tf_op jit(solution)/shard_map/reduce_sum | solution.py:135
  36.5 6.6 %fusion.28 = bf16[3,256,512]{2,1,0:T(8,128)(2,1)S(1)} fusion(bf16[3,4096,512]{2,1,0:T(8,128)(2,1)} %param.9, bf16[256,4096]{1,0:T(8,128)(2,1)S(1)} %copy-done.2, f32[4096]{0:T(1024)S(1)} %copy-done.4, f32[256]{0:T(256)S(1)} %add_rsqrt_fusion), kind=kOutput, calls=%fused_computation.54 | convolution fusion | flops 3225812992 | bytes 15483904 | tf_op jit(solution)/shard_map/td,gdc->gtc/dot_general | solution.py:137
  43.1 3.4 %collective-permute-start = (bf16[3,2,512]{2,1,0:T(2,128)(2,1)S(1)}, bf16[3,2,512]{2,1,0:T(2,128)(2,1)S(1)}, u32[]{:S(2)}, u32[]{:S(2)}) collective-permute-start(bf16[3,2,512]{2,1,0:T(2,128)(2,1)S(1)} %slice.90), channel_id=1, source_target_pairs={{0,4},{4,8},{8,12},{12,16},{16,20},{20,24},{24,28},{1,5},{5,9},{9,... | collective-permute-start | bytes 18440 | tf_op jit(solution)/shard_map/ppermute | solution.py:22
  46.5 1.3 collective-permute-done
  47.8 0.2 maximum_convert_fusion
  48.1 0.5 fusion.21
  48.7 0.5 copy.44
  49.2 19.9 %all_to_all.35 = bf16[2,1,256,512]{3,0,1,2:T(2,128)(2,1)S(1)} all-to-all(bf16[2,1,256,512]{3,0,1,2:T(2,128)(2,1)S(1)} %copy.44), channel_id=1, replica_groups=mesh['ctx'=8,'chan'=4] {'ctx'}, dimensions={2} | all-to-all | bytes 1048576 | tf_op jit(solution)/shard_map/all_to_all | solution.py:99
  69.2 1.1 fusion.26
  70.3 1.1 fusion.27
  71.6 2.5 %copy.48 = bf16[2,2,16,32,512]{4,3,0,1,2:T(8,128)(2,1)} copy(bf16[2,2,16,32,512]{4,2,3,0,1:T(8,128)(2,1)S(1)} %pad_maximum_fusion) | data formatting | bytes 4194304 | tf_op jit(solution)/shard_map/stack | solution.py:85
  74.1 3.6 %all-to-all-start.1 = ((bf16[2,2,16,32,512]{4,3,0,1,2:T(8,128)(2,1)}), bf16[2,2,16,32,512]{4,3,0,1,2:T(8,128)(2,1)S(1)}, u32[]{:S(2)}, u32[]{:S(2)}) async-start(bf16[2,2,16,32,512]{4,3,0,1,2:T(8,128)(2,1)} %copy.48), calls=%async_computation.1 | async-start | bytes 4194304 | tf_op jit(solution)/shard_map/all_to_all | solution.py:103
  78.0 1.0 fusion.72
  79.0 1.0 fusion.70
  80.2 45.4 %all-to-all-done.1 = bf16[2,2,16,32,512]{4,3,0,1,2:T(8,128)(2,1)S(1)} async-done(((bf16[2,2,16,32,512]{4,3,0,1,2:T(8,128)(2,1)}), bf16[2,2,16,32,512]{4,3,0,1,2:T(8,128)(2,1)S(1)}, u32[]{:S(2)}, u32[]{:S(2)}) %all-to-all-start.1) | async-done | bytes 2097184 | tf_op jit(solution)/shard_map/all_to_all | solution.py:103
  125.5 0.6 copy.49
  126.1 0.5 multiply_add_fusion
  126.6 8.0 %fusion.7 = f32[2,2,512,512]{3,2,1,0:T(8,128)S(1)} fusion(f32[2,2,256,512]{3,2,1,0:T(8,128)S(1)} %get-tuple-element.6, f32[2,2,256,512]{3,2,1,0:T(8,128)S(1)} %get-tuple-element.5, f32[256,256]{1,0:T(8,128)S(1)} %get-tuple-element.23, f32[256,256]{1,0:T(8,128)S(1)} %fusion.72, f32[256,256]{1,0:T(8,128)S(1)} %get-tuple-element.22), kind=kOutput, calls=%fused_computation.11 | convolution fusion | flops 6444285952 | bytes 9175040 | tf_op jit(solution)/shard_map/pj,fsjc->fspc/dot_general | solution.py:50
  134.6 0.5 subtract_bitcast_fusion
  135.1 3.8 %multiply_bitcast_fusion = f32[2,512,512]{2,1,0:T(8,128)S(1)} fusion(f32[2,256,512]{2,1,0:T(8,128)S(1)} %get-tuple-element.8, f32[2,256,512]{2,1,0:T(8,128)S(1)} %get-tuple-element.7, f32[256,256]{1,0:T(8,128)S(1)} %get-tuple-element.23, f32[256,256]{1,0:T(8,128)S(1)} %get-tuple-element.22, f32[256,256]{1,0:T(8,128)S(1)} %fusion.72), kind=kOutput, calls=%fused_computation.21 | convolution fusion | flops 3223060480 | bytes 4980736 | tf_op jit(solution)/shard_map/jp,spc->sjc/dot_general | solution.py:68
  138.9 0.3 fusion.43
  139.4 29.6 %all_to_all.36 = bf16[8,2,2,32,512]{4,3,2,1,0:T(8,128)(2,1)S(1)} all-to-all(bf16[8,2,2,32,512]{4,3,2,1,0:T(8,128)(2,1)S(1)} %fusion.69), channel_id=1, replica_groups=mesh['ctx'=8,'chan'=4] {'ctx'}, dimensions={0} | all-to-all | bytes 2097152 | tf_op jit(solution)/shard_map/all_to_all | solution.py:111
  169.1 0.6 fusion.49
  169.7 0.6 fusion.32
  170.4 12.0 %all_to_all.37 = bf16[8,32,512]{2,1,0:T(8,128)(2,1)S(1)} all-to-all(bf16[8,32,512]{2,1,0:T(8,128)(2,1)S(1)} %copy.52), channel_id=1, replica_groups=mesh['ctx'=8,'chan'=4] {'ctx'}, dimensions={0} | all-to-all | bytes 524288 | tf_op jit(solution)/shard_map/all_to_all | solution.py:126
  182.4 2.6 %convolution_convert_fusion = bf16[256,4096]{1,0:T(8,128)(2,1)} fusion(bf16[512,4096]{1,0:T(8,128)(2,1)S(1)} %copy-done.3, f32[3,256,512]{2,1,0:T(8,128)S(1)} %copy-done.1, bf16[256,512]{1,0:T(8,128)(2,1)S(1)} %bitcast.122), kind=kOutput, calls=%fused_computation.3 | convolution fusion | flops 1075183616 | bytes 7077888 | tf_op jit(solution)/shard_map/dot_general | solution.py:173
  185.1 29.6 %reduce-scatter.2.cloned.1.call-done = bf16[256,1024]{1,0:T(8,128)(2,1)} async-done(((bf16[256,4096]{1,0:T(8,128)(2,1)}), bf16[256,1024]{1,0:T(8,128)(2,1)}) %reduce-scatter.2.cloned.1.call-update) | async-done | bytes 524304 | tf_op jit(solution)/shard_map/reduce_scatter | solution.py:174
  (34 shorter events, 1.1 us)
Async XLA Ops:
  6.5 27.7 %all-gather.2.cloned.1.call-start = ((), (), s32[]{:S(2)}) async-start(), calls=%async_computation.5 | async-start | bytes 2621440 | tf_op jit(solution)/shard_map/all_gather | solution.py:133
  9.0 27.5 %copy-start.4 = (f32[4096]{0:T(1024)S(1)}, f32[4096]{0:T(1024)}, u32[]{:S(2)}) copy-start(f32[4096]{0:T(1024)} %param.8) | copy-start | bytes 49156
  34.2 2.3 %copy-start.2 = (bf16[256,4096]{1,0:T(8,128)(2,1)S(1)}, bf16[256,4096]{1,0:T(8,128)(2,1)}, u32[]{:S(2)}) copy-start(bf16[256,4096]{1,0:T(8,128)(2,1)} %all-gather.2.cloned.1.call-done) | copy-start | bytes 6291460
  43.1 4.7 %collective-permute-start = (bf16[3,2,512]{2,1,0:T(2,128)(2,1)S(1)}, bf16[3,2,512]{2,1,0:T(2,128)(2,1)S(1)}, u32[]{:S(2)}, u32[]{:S(2)}) collective-permute-start(bf16[3,2,512]{2,1,0:T(2,128)(2,1)S(1)} %slice.90), channel_id=1, source_target_pairs={{0,4},{4,8},{8,12},{12,16},{16,20},{20,24},{24,28},{1,5},{5,9},{9,... | collective-permute-start | bytes 18440 | tf_op jit(solution)/shard_map/ppermute | solution.py:22
  48.5 20.6 %copy-start = (f32[3,256,512]{2,1,0:T(8,128)}, f32[3,256,512]{2,1,0:T(8,128)S(1)}, u32[]{:S(2)}) copy-start(f32[3,256,512]{2,1,0:T(8,128)S(1)} %fusion.21) | copy-start | bytes 4718596
  74.1 51.4 %all-to-all-start.1 = ((bf16[2,2,16,32,512]{4,3,0,1,2:T(8,128)(2,1)}), bf16[2,2,16,32,512]{4,3,0,1,2:T(8,128)(2,1)S(1)}, u32[]{:S(2)}, u32[]{:S(2)}) async-start(bf16[2,2,16,32,512]{4,3,0,1,2:T(8,128)(2,1)} %copy.48), calls=%async_computation.1 | async-start | bytes 4194304 | tf_op jit(solution)/shard_map/all_to_all | solution.py:103
  77.8 136.9 %reduce-scatter.2.cloned.1.call-start = ((), (), s32[]{:S(2)}) async-start(), calls=%async_computation.6 | async-start | bytes 2621440 | tf_op jit(solution)/shard_map/reduce_scatter | solution.py:174
  139.4 43.0 %copy-start.3 = (bf16[512,4096]{1,0:T(8,128)(2,1)S(1)}, bf16[512,4096]{1,0:T(8,128)(2,1)}, u32[]{:S(2)}) copy-start(bf16[512,4096]{1,0:T(8,128)(2,1)} %param.13) | copy-start | bytes 12582916
  169.1 13.3 %copy-start.1 = (f32[3,256,512]{2,1,0:T(8,128)S(1)}, f32[3,256,512]{2,1,0:T(8,128)}, u32[]{:S(2)}) copy-start(f32[3,256,512]{2,1,0:T(8,128)} %copy-done) | copy-start | bytes 4718596
Sparse Core Ops, SparseCore 0:
  8.9 25.2 all-gather.1
  185.2 29.4 reduce-scatter.1
